TPU v7x, 32 devices: a whole 2x2x4 slice. The times are simulated.
32 devices in a mesh: mp: 2 (over y), survey: 16 (over z, x, core).
Axes of the slice: x: 2, y: 2, z: 4, core: 2. Of those that a mesh axis runs over, the one named last changes fastest.
Arguments:
- model: bfloat16 [64, 64, 128], P(('mp', 'survey')), may hold values from -6 to 6
- observed: bfloat16 [32, 64, 128], P(('mp', 'survey')), may hold values from -6 to 6
- weights: bfloat16 [32, 64, 128], P(('mp', 'survey')), may hold values from 0.29882812 to 3
- sensitivity: bfloat16 [2, 2048, 128, 128], P('mp', 'survey'), may hold values from -0.046875 to 0.046875
- block_rows: int32 [2, 2048], P('mp', 'survey'), may hold values from 0 to 15
- block_cols: int32 [2, 2048], P('mp', 'survey'), may hold values from 0 to 3
- block_count: int32 [2, 16], P('mp', 'survey'), may hold values from 32 to 128, as said below
Outputs:
- gradient: float32 [64, 64, 128], P(('mp', 'survey'))
Inputs may be any that keep to these rules, and one draw needn't show every extreme that they name: `block_count`: some device uses all 128 slots.
All inputs are finite; a program needn't handle non-finite values.
Results may differ from a plain program's by a relative error of at most 0.0017.
Values may be sent and summed in bfloat16 or wider, within the bound.
A program may use at most 64 MiB of HBM per device.

v0:
```python
import jax
import jax.numpy as jnp
from jax import lax
from jax.sharding import PartitionSpec as P

SMOOTH = 0.5


def smoothing(model):
    field_f32 = model.astype(jnp.float32)
    earlier = jnp.concatenate([field_f32[:, :1], field_f32[:, :-1]], axis=1)
    later_step = jnp.concatenate([field_f32[:, 1:], field_f32[:, -1:]], axis=1)
    return SMOOTH * (2.0 * field_f32 - earlier - later_step)


def collect(target_ids, in_use, terms, count):
    spare_ids = jnp.where(in_use, target_ids, count)
    summed = jax.ops.segment_sum(terms, spare_ids, num_segments=count + 1)
    return summed[:count]


def on_device(model, observed, weights, sensitivity, block_rows, block_cols, block_count):
    blocks = sensitivity[0]
    row_ids = block_rows[0]
    col_ids = block_cols[0]
    slots = blocks.shape[0]
    in_use = jnp.arange(slots, dtype=jnp.int32) < block_count[0, 0]
    group_rows = observed.shape[0] * lax.axis_size("survey")
    slab = lax.all_gather(model, "mp", axis=0, tiled=True)
    slab_rows = slab.shape[0]
    picked = jnp.take(slab, col_ids, axis=0)
    terms = jnp.einsum("ktc,krc->ktr", picked, blocks, preferred_element_type=jnp.float32)
    partial_value = collect(row_ids, in_use, terms, group_rows)
    summed = lax.psum(partial_value, "survey")
    seen_data, data_weight = (
        lax.all_gather(observed, "survey", axis=0, tiled=True),
        lax.all_gather(weights, "survey", axis=0, tiled=True),
    )
    residual = (data_weight.astype(jnp.float32) * (summed - seen_data.astype(jnp.float32))).astype(
        jnp.bfloat16
    )
    resid_rows = jnp.take(residual, row_ids, axis=0)
    back_terms = jnp.einsum("ktr,krc->ktc", resid_rows, blocks, preferred_element_type=jnp.float32)
    gradient_slab = collect(col_ids, in_use, back_terms, slab_rows)
    owned = lax.psum_scatter(gradient_slab, "mp", scatter_dimension=0, tiled=True)
    return owned + smoothing(model)


def solution(mesh):
    in_specs = (
        P(("mp", "survey"), None, None),
        P(("mp", "survey"), None, None),
        P(("mp", "survey"), None, None),
        P("mp", "survey", None, None),
        P("mp", "survey"),
        P("mp", "survey"),
        P("mp", "survey"),
    )
    out_specs = P(("mp", "survey"), None, None)
    return jax.shard_map(
        on_device, mesh=mesh, in_specs=in_specs, out_specs=out_specs, check_vma=False
    )
```

profile of v0, /device:TPU:0, one launch (start us, length us, event | category | flops | bytes accessed | tf_op | source)
XLA Modules:
  0.0 170.1 jit_solution(15884253694293784097)
XLA Ops:
  6.5 0.0 all-reduce.2.cloned.1.call-start
  7.2 0.7 compare_and_fusion
  7.9 0.7 fusion.15
  8.5 5.8 %all_gather.10 = bf16[4,64,128]{2,1,0:T(8,128)(2,1)S(1)} all-gather(bf16[2,64,128]{2,1,0:T(8,128)(2,1)} %param.7), channel_id=1, replica_groups=mesh['mp'=2,'survey'=16] {'mp'}, dimensions={0}, use_global_device_ids=true | all-gather | bytes 98304 | tf_op jit(solution)/shard_map/all_gather | solution.py:29
  14.3 0.0 copy-start.3
  14.3 0.9 gather_fusion
  15.3 0.0 copy-done.3
  15.3 7.1 %fusion.2 = f32[128,64,128]{2,1,0:T(8,128)} fusion(bf16[1,128,128,128]{3,2,1,0:T(8,128)(2,1)} %param.10, bf16[128,64,128]{2,1,0:T(8,128)(2,1)S(1)} %gather_fusion, pred[128]{0:T(512)(128)(4,1)S(1)} %compare_and_fusion), kind=kOutput, calls=%fused_computation.6 | convolution fusion | flops 269484032 | bytes 10485888 | tf_op jit(solution)/shard_map/ktc,krc->ktr/dot_general | solution.py:32
  22.4 0.0 copy-start.1
  22.4 0.0 copy-start.2
  22.4 13.5 %scatter_fusion = f32[17,64,128]{2,1,0:T(8,128)S(1)} fusion(f32[17,64,128]{2,1,0:T(8,128)S(1)} %broadcast_in_dim.36, s32[128]{0:T(128)S(1)} %get-tuple-element.10, f32[128,64,128]{2,1,0:T(8,128)} %fusion.2), kind=kCustom, calls=%fused_computation.2 | custom fusion | flops 1048576 | bytes 12583424 | tf_op jit(solution)/shard_map/scatter-add | solution.py:18
  36.0 0.8 slice.28
  36.8 0.0 all-reduce.2.cloned.1.call-update
  36.8 0.0 reduce-scatter.2.cloned.1.call-start
  36.9 0.0 copy-done.1
  36.9 23.0 %all_gather.11 = bf16[16,64,128]{2,1,0:T(8,128)(2,1)S(1)} all-gather(bf16[1,64,128]{2,1,0:T(8,128)(2,1)S(1)} %copy-done.1), channel_id=1, replica_groups=mesh['mp'=2,'survey'=16] {'survey'}, dimensions={0}, use_global_device_ids=true | all-gather | bytes 278528 | tf_op jit(solution)/shard_map/all_gather | solution.py:36
  59.9 0.0 copy-done.2
  59.9 18.2 %all_gather.9 = bf16[16,64,128]{2,1,0:T(8,128)(2,1)S(1)} all-gather(bf16[1,64,128]{2,1,0:T(8,128)(2,1)S(1)} %copy-done.2), channel_id=1, replica_groups=mesh['mp'=2,'survey'=16] {'survey'}, dimensions={0}, use_global_device_ids=true | all-gather | bytes 278528 | tf_op jit(solution)/shard_map/all_gather | solution.py:37
  78.1 50.9 %all-reduce.2.cloned.1.call-done = f32[16,64,128]{2,1,0:T(8,128)} async-done(((f32[16,64,128]{2,1,0:T(8,128)}), f32[16,64,128]{2,1,0:T(8,128)}) %all-reduce.2.cloned.1.call-update) | async-done | bytes 524304 | tf_op jit(solution)/shard_map/psum | solution.py:34
  129.1 1.1 multiply_convert_fusion
  130.2 1.0 gather_fusion.1
  131.2 5.4 %fusion = f32[128,64,128]{2,1,0:T(8,128)} fusion(bf16[1,128,128,128]{3,2,1,0:T(8,128)(2,1)} %param.10, bf16[128,64,128]{2,1,0:T(8,128)(2,1)S(1)} %gather_fusion.1, pred[128]{0:T(512)(128)(4,1)S(1)} %compare_and_fusion.1), kind=kOutput, calls=%fused_computation.4 | convolution fusion | flops 269484032 | bytes 10485888 | tf_op jit(solution)/shard_map/ktr,krc->ktc/dot_general | solution.py:43
  136.6 0.0 copy-start
  136.6 13.6 %scatter_fusion.1 = f32[5,64,128]{2,1,0:T(8,128)S(1)} fusion(f32[5,64,128]{2,1,0:T(8,128)S(1)} %broadcast_in_dim.33, s32[128]{0:T(128)S(1)} %get-tuple-element.12, f32[128,64,128]{2,1,0:T(8,128)} %fusion), kind=kCustom, calls=%fused_computation.3 | custom fusion | flops 1048576 | bytes 12583424 | tf_op jit(solution)/shard_map/scatter-add | solution.py:18
  150.2 0.7 slice.29
  150.9 0.0 reduce-scatter.2.cloned.1.call-update
  150.9 0.0 copy-done
  150.9 10.9 %reduce-scatter.2.cloned.1.call-done = f32[2,64,128]{2,1,0:T(8,128)} async-done(((f32[4,64,128]{2,1,0:T(8,128)}), f32[2,64,128]{2,1,0:T(8,128)}) %reduce-scatter.2.cloned.1.call-update) | async-done | bytes 65552 | tf_op jit(solution)/shard_map/reduce_scatter | solution.py:45
  161.8 1.5 fusion.12
  (8 shorter events, 0.1 us)
Async XLA Ops:
  6.5 122.5 %all-reduce.2.cloned.1.call-start = ((), (), s32[]{:S(2)}) async-start(), calls=%async_computation.1 | async-start | bytes 1048576 | tf_op jit(solution)/shard_map/psum | solution.py:34
  14.3 1.0 copy-start.3
  22.4 14.5 %copy-start.1 = (bf16[1,64,128]{2,1,0:T(8,128)(2,1)S(1)}, bf16[1,64,128]{2,1,0:T(8,128)(2,1)}, u32[]{:S(2)}) copy-start(bf16[1,64,128]{2,1,0:T(8,128)(2,1)} %param.8) | copy-start | bytes 49156
  22.4 37.5 %copy-start.2 = (bf16[1,64,128]{2,1,0:T(8,128)(2,1)S(1)}, bf16[1,64,128]{2,1,0:T(8,128)(2,1)}, u32[]{:S(2)}) copy-start(bf16[1,64,128]{2,1,0:T(8,128)(2,1)} %param.9) | copy-start | bytes 49156
  36.8 125.0 %reduce-scatter.2.cloned.1.call-start = ((), (), s32[]{:S(2)}) async-start(), calls=%async_computation.2 | async-start | bytes 196608 | tf_op jit(solution)/shard_map/reduce_scatter | solution.py:45
  136.6 14.3 %copy-start = (bf16[2,64,128]{2,1,0:T(8,128)(2,1)S(1)}, bf16[2,64,128]{2,1,0:T(8,128)(2,1)}, u32[]{:S(2)}) copy-start(bf16[2,64,128]{2,1,0:T(8,128)(2,1)} %param.7) | copy-start | bytes 98308
Sparse Core Ops, SparseCore 0:
  37.0 92.0 all-reduce.1
  151.0 10.7 reduce-scatter.1
where the time goes:
time: 171 us; the launch traced here: 170 us
  waiting for transfers between devices  61.9 us (36%)
  blocking collectives  47 us (27%)
  other arithmetic  31.1 us (18%)
  between operations  14.2 us (8%)
  matrix products  12.5 us (7%)
  local copies, waits for them, and re-layouts  3.49 us (2%)
    psum x1, waiting for transfers between devices, on_device(): summed = lax.psum(partial_value, 'survey')  50.9 us
    scatter-add x2, other arithmetic, collect(): summed = jax.ops.segment_sum(terms, spare_ids, num_segments=count + 1)  27.1 us
    all_gather x1, blocking collectives, on_device(): lax.all_gather(observed, 'survey', axis=0, tiled=True)  23 us
    all_gather x1, blocking collectives, on_device(): lax.all_gather(weights, 'survey', axis=0, tiled=True)  18.2 us
    reduce_scatter x1, waiting for transfers between devices, on_device(): lax.psum_scatter(gradient_slab, 'mp', scatter_dimension=0, tiled=True)  10.9 us
    dot_general x1, matrix products, on_device(): jnp.einsum('ktc,krc->ktr', picked, blocks, preferred_element_type=jnp.flo...  7.05 us
    all_gather x1, blocking collectives, on_device(): slab = lax.all_gather(model, 'mp', axis=0, tiled=True)  5.79 us
    dot_general x1, matrix products, on_device(): jnp.einsum('ktr,krc->ktc', resid_rows, blocks, preferred_element_type=jnp...  5.4 us
  transfers between devices with their start and end apart: 2, of which 2 were waited for; matrix products, arithmetic and copies ran while one was open for 0% of the time, Pallas kernels for 0%

commit v1 on v0

--- a/solution.py
+++ b/solution.py
@@ -4,6 +4,11 @@
 from jax.sharding import PartitionSpec as P
 
 SMOOTH = 0.5
+
+
+def gather_and_add(x, name):
+    shards = lax.all_gather(x, name)
+    return jnp.sum(shards, axis=0)
 
 
 def smoothing(model):
@@ -31,7 +36,7 @@
     picked = jnp.take(slab, col_ids, axis=0)
     terms = jnp.einsum("ktc,krc->ktr", picked, blocks, preferred_element_type=jnp.float32)
     partial_value = collect(row_ids, in_use, terms, group_rows)
-    summed = lax.psum(partial_value, "survey")
+    summed = gather_and_add(partial_value, "survey")
     seen_data, data_weight = (
         lax.all_gather(observed, "survey", axis=0, tiled=True),
         lax.all_gather(weights, "survey", axis=0, tiled=True),

time: 171 us -> 158 us (0.924)
  waiting for transfers between devices: 61.9 us -> 44.2 us
  other arithmetic: 31.1 us -> 34.3 us
    psum x1 -> x0, waiting for transfers between devices: 50.9 us -> none  [on_device(): summed = lax.psum(partial_value, 'survey')]
    all_gather x0 -> x1, waiting for transfers between devices: none -> 35.3 us  [gather_and_add(): shards = lax.all_gather(x, name)]
    all_gather x1, blocking collectives: 18.2 us -> 23.6 us  [on_device(): lax.all_gather(weights, 'survey', axis=0, tiled=True)]
    reduce_sum x0 -> x1, other arithmetic: none -> 4.24 us  [gather_and_add(): return jnp.sum(shards, axis=0)]
    all_gather x1, blocking collectives: 23 us -> 19.1 us  [on_device(): lax.all_gather(observed, 'survey', axis=0, tiled=True)]
    reduce_scatter x1, waiting for transfers between devices: 10.9 us -> 8.87 us  [on_device(): lax.psum_scatter(gradient_slab, 'mp', scatter_dimension=0, tiled=True)]
where the time goes in v1:
time: 158 us; the launch traced here: 157 us
  blocking collectives  48.4 us (31%)
  waiting for transfers between devices  44.2 us (28%)
  other arithmetic  34.3 us (22%)
  between operations  14.2 us (9%)
  matrix products  12.5 us (8%)
  local copies, waits for them, and re-layouts  3.54 us (2%)
    all_gather x1, waiting for transfers between devices, gather_and_add(): shards = lax.all_gather(x, name)  35.3 us
    scatter-add x2, other arithmetic, collect(): summed = jax.ops.segment_sum(terms, spare_ids, num_segments=count + 1)  27.1 us
    all_gather x1, blocking collectives, on_device(): lax.all_gather(weights, 'survey', axis=0, tiled=True)  23.6 us
    all_gather x1, blocking collectives, on_device(): lax.all_gather(observed, 'survey', axis=0, tiled=True)  19.1 us
    reduce_scatter x1, waiting for transfers between devices, on_device(): lax.psum_scatter(gradient_slab, 'mp', scatter_dimension=0, tiled=True)  8.87 us
    dot_general x1, matrix products, on_device(): jnp.einsum('ktc,krc->ktr', picked, blocks, preferred_element_type=jnp.flo...  7.05 us
    all_gather x1, blocking collectives, on_device(): slab = lax.all_gather(model, 'mp', axis=0, tiled=True)  5.79 us
    dot_general x1, matrix products, on_device(): jnp.einsum('ktr,krc->ktc', resid_rows, blocks, preferred_element_type=jnp...  5.4 us
  transfers between devices with their start and end apart: 2, of which 2 were waited for; matrix products, arithmetic and copies ran while one was open for 0% of the time, Pallas kernels for 0%

profile of v1, /device:TPU:0, one launch (start us, length us, event | category | flops | bytes accessed | tf_op | source)
XLA Modules:
  0.0 157.2 jit_solution(17542198511322169304)
XLA Ops:
  6.5 0.0 copy-start.3
  6.5 0.0 all-gather.3.cloned.1.call-start
  7.2 0.7 compare_and_fusion
  7.9 0.7 fusion.15
  8.5 5.8 %all_gather.16 = bf16[4,64,128]{2,1,0:T(8,128)(2,1)S(1)} all-gather(bf16[2,64,128]{2,1,0:T(8,128)(2,1)} %param.7), channel_id=1, replica_groups=mesh['mp'=2,'survey'=16] {'mp'}, dimensions={0}, use_global_device_ids=true | all-gather | bytes 98304 | tf_op jit(solution)/shard_map/all_gather | solution.py:34
  14.3 0.9 gather_fusion
  15.3 0.0 copy-done.3
  15.3 7.1 %fusion.2 = f32[128,64,128]{2,1,0:T(8,128)} fusion(bf16[1,128,128,128]{3,2,1,0:T(8,128)(2,1)} %param.10, bf16[128,64,128]{2,1,0:T(8,128)(2,1)S(1)} %gather_fusion, pred[128]{0:T(512)(128)(4,1)S(1)} %compare_and_fusion), kind=kOutput, calls=%fused_computation.6 | convolution fusion | flops 269484032 | bytes 10485888 | tf_op jit(solution)/shard_map/ktc,krc->ktr/dot_general | solution.py:37
  22.4 0.0 copy-start.1
  22.4 0.0 copy-start.2
  22.4 13.5 %scatter_fusion = f32[17,64,128]{2,1,0:T(8,128)S(1)} fusion(f32[17,64,128]{2,1,0:T(8,128)S(1)} %broadcast_in_dim.36, s32[128]{0:T(128)S(1)} %get-tuple-element.10, f32[128,64,128]{2,1,0:T(8,128)} %fusion.2), kind=kCustom, calls=%fused_computation.2 | custom fusion | flops 1048576 | bytes 12583424 | tf_op jit(solution)/shard_map/scatter-add | solution.py:23
  36.0 0.9 slice.28
  36.9 0.0 all-gather.3.cloned.1.call-update
  36.9 0.0 reduce-scatter.2.cloned.1.call-start
  37.0 0.0 copy-done.1
  37.0 23.6 %all_gather.15 = bf16[16,64,128]{2,1,0:T(8,128)(2,1)S(1)} all-gather(bf16[1,64,128]{2,1,0:T(8,128)(2,1)S(1)} %copy-done.1), channel_id=1, replica_groups=mesh['mp'=2,'survey'=16] {'survey'}, dimensions={0}, use_global_device_ids=true | all-gather | bytes 278528 | tf_op jit(solution)/shard_map/all_gather | solution.py:42
  60.5 0.0 copy-done.2
  60.5 19.1 %all_gather.19 = bf16[16,64,128]{2,1,0:T(8,128)(2,1)S(1)} all-gather(bf16[1,64,128]{2,1,0:T(8,128)(2,1)S(1)} %copy-done.2), channel_id=1, replica_groups=mesh['mp'=2,'survey'=16] {'survey'}, dimensions={0}, use_global_device_ids=true | all-gather | bytes 278528 | tf_op jit(solution)/shard_map/all_gather | solution.py:41
  79.6 35.3 %all-gather.3.cloned.1.call-done = f32[256,64,128]{2,1,0:T(8,128)} async-done(((f32[16,64,128]{2,1,0:T(8,128)}), f32[256,64,128]{2,1,0:T(8,128)}) %all-gather.3.cloned.1.call-update) | async-done | bytes 8388624 | tf_op jit(solution)/shard_map/all_gather | solution.py:10
  114.9 4.2 %reduce_sum.9 = f32[16,64,128]{2,1,0:T(8,128)S(1)} reduce(f32[16,16,64,128]{3,2,1,0:T(8,128)} %bitcast.27, f32[]{:T(128)} %constant.12.clone.1), dimensions={0}, to_apply=%region_1.2 | reduce | flops 1966080 | bytes 8912900 | tf_op jit(solution)/shard_map/reduce_sum | solution.py:11
  119.2 0.1 multiply_convert_fusion
  119.3 1.0 gather_fusion.1
  120.2 5.4 %fusion = f32[128,64,128]{2,1,0:T(8,128)} fusion(bf16[1,128,128,128]{3,2,1,0:T(8,128)(2,1)} %param.10, bf16[128,64,128]{2,1,0:T(8,128)(2,1)S(1)} %gather_fusion.1, pred[128]{0:T(512)(128)(4,1)S(1)} %compare_and_fusion.1), kind=kOutput, calls=%fused_computation.4 | convolution fusion | flops 269484032 | bytes 10485888 | tf_op jit(solution)/shard_map/ktr,krc->ktc/dot_general | solution.py:48
  125.7 0.0 copy-start
  125.7 13.6 %scatter_fusion.1 = f32[5,64,128]{2,1,0:T(8,128)S(1)} fusion(f32[5,64,128]{2,1,0:T(8,128)S(1)} %broadcast_in_dim.33, s32[128]{0:T(128)S(1)} %get-tuple-element.12, f32[128,64,128]{2,1,0:T(8,128)} %fusion), kind=kCustom, calls=%fused_computation.3 | custom fusion | flops 1048576 | bytes 12583424 | tf_op jit(solution)/shard_map/scatter-add | solution.py:23
  139.3 0.7 slice.29
  139.9 0.0 reduce-scatter.2.cloned.1.call-update
  139.9 0.0 copy-done
  140.0 8.9 %reduce-scatter.2.cloned.1.call-done = f32[2,64,128]{2,1,0:T(8,128)} async-done(((f32[4,64,128]{2,1,0:T(8,128)}), f32[2,64,128]{2,1,0:T(8,128)}) %reduce-scatter.2.cloned.1.call-update) | async-done | bytes 65552 | tf_op jit(solution)/shard_map/reduce_scatter | solution.py:50
  148.9 1.5 fusion.12
  (8 shorter events, 0.1 us)
Async XLA Ops:
  6.5 8.8 %copy-start.3 = (s32[1,128]{1,0:T(1,128)S(1)}, s32[1,128]{1,0:T(1,128)}, u32[]{:S(2)}) copy-start(s32[1,128]{1,0:T(1,128)} %param.11) | copy-start | bytes 1540
  6.5 108.4 %all-gather.3.cloned.1.call-start = ((), (), s32[]{:S(2)}) async-start(), calls=%async_computation.2 | async-start | bytes 8912896 | tf_op jit(solution)/shard_map/all_gather | solution.py:10
  22.4 14.6 %copy-start.1 = (bf16[1,64,128]{2,1,0:T(8,128)(2,1)S(1)}, bf16[1,64,128]{2,1,0:T(8,128)(2,1)}, u32[]{:S(2)}) copy-start(bf16[1,64,128]{2,1,0:T(8,128)(2,1)} %param.9) | copy-start | bytes 49156
  22.4 38.1 %copy-start.2 = (bf16[1,64,128]{2,1,0:T(8,128)(2,1)S(1)}, bf16[1,64,128]{2,1,0:T(8,128)(2,1)}, u32[]{:S(2)}) copy-start(bf16[1,64,128]{2,1,0:T(8,128)(2,1)} %param.8) | copy-start | bytes 49156
  36.9 112.0 %reduce-scatter.2.cloned.1.call-start = ((), (), s32[]{:S(2)}) async-start(), calls=%async_computation.1 | async-start | bytes 196608 | tf_op jit(solution)/shard_map/reduce_scatter | solution.py:50
  125.7 14.3 %copy-start = (bf16[2,64,128]{2,1,0:T(8,128)(2,1)S(1)}, bf16[2,64,128]{2,1,0:T(8,128)(2,1)}, u32[]{:S(2)}) copy-start(bf16[2,64,128]{2,1,0:T(8,128)(2,1)} %param.7) | copy-start | bytes 98308
Sparse Core Ops, SparseCore 0:
  37.0 77.8 all-gather.2
  140.1 8.7 reduce-scatter.1
